TPU v7x, 32 devices: a whole 2x2x4 slice. The times are simulated.
32 devices in a mesh: shard: 4 (over z), ctx: 4 (over y, x), tp: 2 (over core).
Axes of the slice: x: 2, y: 2, z: 4, core: 2. Of those that a mesh axis runs over, the one named last changes fastest.
Arguments:
- tokens: bfloat16 [4, 4096, 1024], P('shard', 'ctx'), may hold values from -6 to 6
- lengths: int32 [4], P('shard'), may hold values from 1024 to 4096, as said below
- routes: int32 [4, 4096, 1], P('shard', 'ctx'), may hold values from 0 to 15
- query_key_value_weight: bfloat16 [3, 1024, 1024], P(None, ('shard', 'ctx'), 'tp'), may hold values from -0.1875 to 0.1875
- context_blend_linear_map: bfloat16 [1024, 1024], P(('shard', 'ctx'), 'tp'), may hold values from -3 to 3
- router: bfloat16 [1024, 16], P(('shard', 'ctx')), may hold values from -0.09375 to 0.09375
- gain_one: bfloat16 [1024], P(('shard', 'ctx')), may hold values from 0.5 to 1.5
- gain_two: bfloat16 [1024], P(('shard', 'ctx')), may hold values from 0.5 to 1.5
- w_in: bfloat16 [16, 1024, 4096], P(('shard', 'ctx'), None, 'tp'), may hold values from -0.1875 to 0.1875
- w_out: bfloat16 [16, 4096, 1024], P(('shard', 'ctx'), 'tp'), may hold values from -1.5 to 1.5
- cotangent: bfloat16 [4, 4096, 1024], P('shard', 'ctx'), may hold values from -6 to 6
Outputs:
- output: bfloat16 [4, 4096, 1024], P('shard', 'ctx')
- grad_tokens: float32 [4, 4096, 1024], P('shard', 'ctx')
- grad_w_qkv: float32 [3, 1024, 1024], P(None, ('shard', 'ctx'), 'tp')
- grad_attn_proj: float32 [1024, 1024], P(('shard', 'ctx'), 'tp')
- grad_router: float32 [1024, 16], P(('shard', 'ctx'))
- grad_gain_one: float32 [1024], P(('shard', 'ctx'))
- grad_gain_two: float32 [1024], P(('shard', 'ctx'))
- grad_w_in: float32 [16, 1024, 4096], P(('shard', 'ctx'), None, 'tp')
- grad_w_out: float32 [16, 4096, 1024], P(('shard', 'ctx'), 'tp')
Inputs may be any that keep to these rules, and one draw needn't show every extreme that they name: `lengths`: at least one slot has all 4096 positions used.
All inputs are finite; a program needn't handle non-finite values.
Results may differ from a plain program's by a relative error of at most 0.03.
Values may be sent and summed in bfloat16 or wider, within the bound.
A program may use at most 256 MiB of HBM per device.

v0:
```python
import math
import jax
import jax.numpy as jnp
from jax import lax
from jax.sharding import PartitionSpec as P

HEAD_DIM = 64
epsilon = 1e-05
masked_score = -1e30
key_block = 512


def norm_parts(values, gain):
    center = values - jnp.mean(values, axis=-1, keepdims=True)
    multiplier_coefficient = lax.rsqrt(jnp.mean(center * center, axis=-1, keepdims=True) + epsilon)
    normed = center * multiplier_coefficient
    return (normed * gain, normed, multiplier_coefficient)


def norm_back(grad, normed, multiplier_coefficient, gain):
    scaled = grad * gain
    inner = (
        scaled
        - jnp.mean(scaled, axis=-1, keepdims=True)
        - normed * jnp.mean(scaled * normed, axis=-1, keepdims=True)
    )
    return (inner * multiplier_coefficient, jnp.sum(grad * normed, axis=0))


def score_block(query, block, begin, query_places, lengths, heads):
    slots, block_len, twice = block.shape
    half = twice // 2
    keys = block[:, :, :half].reshape(slots, block_len, heads, HEAD_DIM)
    values = block[:, :, half:].reshape(slots, block_len, heads, HEAD_DIM)
    key_places = begin + jnp.arange(block_len, dtype=jnp.int32)
    allowed = (key_places[None, None, :] <= query_places[None, :, None]) & (
        key_places[None, None, :] < lengths[:, None, None]
    )
    scores = jnp.einsum(
        "sqhd,skhd->sqhk", query, keys, preferred_element_type=jnp.float32
    ) * HEAD_DIM ** (-0.5)
    return (keys, values, allowed[:, :, None, :], scores)


def contract_rows(left, right):
    return lax.dot_general(
        left, right, (((0,), (0,)), ((), ())), preferred_element_type=jnp.float32
    )


def contract_cols(left, right):
    return lax.dot_general(
        left, right, (((1,), (1,)), ((), ())), preferred_element_type=jnp.float32
    )


def local(
    tokens,
    lengths,
    routes,
    query_key_value_weight,
    context_blend_linear_map,
    router,
    gain_one,
    gain_two,
    w_in,
    w_out,
    cotangent,
):
    slots, local_len, width = tokens.shape
    count = slots * local_len
    head_width = query_key_value_weight.shape[2]
    heads = head_width // HEAD_DIM
    experts = router.shape[1]
    capacity = max(2, (5 * count + 4 * experts - 1) // (4 * experts))
    scale = HEAD_DIM ** (-0.5)
    ctx_rank = lax.axis_index("ctx")
    query_places = ctx_rank * local_len + jnp.arange(local_len, dtype=jnp.int32)
    full_qkv, full_proj, full_router, full_one, full_two = (
        lax.all_gather(query_key_value_weight, ("shard", "ctx"), axis=1, tiled=True),
        lax.all_gather(context_blend_linear_map, ("shard", "ctx"), axis=0, tiled=True),
        lax.all_gather(router, ("shard", "ctx"), axis=0, tiled=True),
        lax.all_gather(gain_one, ("shard", "ctx"), axis=0, tiled=True),
        lax.all_gather(gain_two, ("shard", "ctx"), axis=0, tiled=True),
    )
    scale_one = full_one.astype(jnp.float32)
    scale_two = full_two.astype(jnp.float32)
    inputs = tokens.astype(jnp.float32).reshape(count, width)
    normed_one, unit_one, inverse_one = norm_parts(inputs, scale_one)
    first_part = normed_one.astype(jnp.bfloat16)
    projected_rows = jnp.einsum(
        "td,kdf->tkf", first_part, full_qkv, preferred_element_type=jnp.float32
    ).astype(jnp.bfloat16)
    query = projected_rows[:, 0].reshape(slots, local_len, heads, HEAD_DIM)
    pairs = projected_rows[:, 1:].reshape(slots, local_len, 2 * head_width)
    start_state = (
        jnp.full((slots, local_len, heads), masked_score, jnp.float32),
        jnp.zeros((slots, local_len, heads), jnp.float32),
        jnp.zeros((slots, local_len, heads, HEAD_DIM), jnp.float32),
    )
    piece = lax.all_gather(pairs, "ctx", axis=1, tiled=True)
    piece_len = piece.shape[1]
    step_size = math.gcd(piece_len, key_block)

    def inner(number, state):
        top, total, accum = state
        offset = number * step_size
        block = lax.dynamic_slice_in_dim(piece, offset, step_size, 1)
        keys, values, allowed, scores = score_block(
            query, block, offset, query_places, lengths, heads
        )
        scores = jnp.where(allowed, scores, masked_score)
        new_top = jnp.maximum(top, jnp.max(scores, axis=-1))
        factor = jnp.exp(top - new_top)
        weights = jnp.where(allowed, jnp.exp(scores - new_top[..., None]), 0.0)
        total = total * factor + jnp.sum(weights, axis=-1)
        accum = accum * factor[..., None] + jnp.einsum(
            "sqhk,skhd->sqhd",
            weights.astype(jnp.bfloat16),
            values,
            preferred_element_type=jnp.float32,
        )
        return (new_top, total, accum)

    top, total, accum = lax.fori_loop(0, piece_len // step_size, inner, start_state)
    log_total = top + jnp.log(total)
    blended_layer_yield = (accum / total[..., None]).astype(jnp.bfloat16)
    mixed_rows = blended_layer_yield.reshape(count, head_width)
    partial_branch = jnp.einsum(
        "tf,df->td", mixed_rows, full_proj, preferred_element_type=jnp.float32
    )
    expert_path_yield = lax.psum(partial_branch.astype(jnp.bfloat16), "tp").astype(jnp.float32)
    middle = inputs + expert_path_yield
    normed_two, unit_two, inverse_two = norm_parts(middle, scale_two)
    second_part = normed_two.astype(jnp.bfloat16)
    router_logits = jnp.dot(second_part, full_router, preferred_element_type=jnp.float32)
    probs = jax.nn.softmax(router_logits, axis=-1)
    route = routes.reshape(count)
    valid = (query_places[None, :] < lengths[:, None]).reshape(count)
    expert_ids = jnp.arange(experts, dtype=jnp.int32)
    route_hot = route[:, None] == expert_ids[None, :]
    gate = jnp.sum(jnp.where(route_hot, probs, 0.0), axis=1)
    counted = (route_hot & valid[:, None]).astype(jnp.int32)
    earlier = jnp.cumsum(counted, axis=0) - counted
    place = jnp.sum(earlier * counted, axis=1)
    kept = valid & (place < capacity)
    target = jnp.where(kept, route * capacity + place, experts * capacity)
    send = (
        jnp.zeros((experts * capacity + 1, width), jnp.bfloat16)
        .at[target]
        .set(second_part)[:-1]
        .reshape(experts, capacity, width)
    )
    arrived_here = lax.all_to_all(send, ("shard", "ctx"), split_axis=0, concat_axis=0, tiled=True)
    sources, items, _ = arrived_here.shape
    arrived_rows = arrived_here.reshape(sources * items, width)
    pre = jnp.dot(arrived_rows, w_in[0], preferred_element_type=jnp.float32)
    hidden = jax.nn.gelu(pre).astype(jnp.bfloat16)
    partial_out = jnp.dot(hidden, w_out[0], preferred_element_type=jnp.float32)
    summed = lax.psum(partial_out.astype(jnp.bfloat16), "tp")
    going_back = lax.all_to_all(
        summed.reshape(sources, items, width),
        ("shard", "ctx"),
        split_axis=0,
        concat_axis=0,
        tiled=True,
    )
    pre_act = pre.reshape(sources, items, pre.shape[1])
    fetched = jnp.concatenate(
        [going_back.reshape(experts * capacity, width), jnp.zeros((1, width), jnp.bfloat16)], axis=0
    )[target]
    fetched_value = fetched.astype(jnp.float32)
    kept_value = kept.astype(jnp.float32)
    valid_value = valid.astype(jnp.float32)
    weighted_gate = kept_value * gate
    moe = weighted_gate[:, None] * fetched_value
    output = (
        (valid_value[:, None] * (middle + moe))
        .astype(jnp.bfloat16)
        .reshape(slots, local_len, width)
    )
    grad_out = valid_value[:, None] * cotangent.astype(jnp.float32).reshape(count, width)
    grad_fetched = (weighted_gate[:, None] * grad_out).astype(jnp.bfloat16)
    grad_send = (
        jnp.zeros((experts * capacity + 1, width), jnp.bfloat16)
        .at[target]
        .set(grad_fetched)[:-1]
        .reshape(experts, capacity, width)
    )
    grad_arrived = lax.all_to_all(
        grad_send, ("shard", "ctx"), split_axis=0, concat_axis=0, tiled=True
    )
    arrived_rows = arrived_here.reshape(-1, width)
    grad_rows = grad_arrived.reshape(-1, width)
    pre_rows = pre_act.reshape(arrived_rows.shape[0], pre_act.shape[2])
    hidden_rows = jax.nn.gelu(pre_rows).astype(jnp.bfloat16)
    grad_w_out = contract_rows(hidden_rows, grad_rows)[None]
    grad_hidden = contract_cols(grad_rows, w_out[0])
    unused_value, gelu_back = jax.vjp(jax.nn.gelu, pre_rows)
    grad_pre = gelu_back(grad_hidden)[0].astype(jnp.bfloat16)
    grad_w_in = contract_rows(arrived_rows, grad_pre)[None]
    partial_grad = contract_cols(grad_pre, w_in[0])
    grad_dispatched = lax.psum(partial_grad.astype(jnp.bfloat16), "tp")
    grad_home = lax.all_to_all(
        grad_dispatched.reshape(arrived_here.shape),
        ("shard", "ctx"),
        split_axis=0,
        concat_axis=0,
        tiled=True,
    )
    grad_home_rows = jnp.concatenate(
        [grad_home.reshape(experts * capacity, width), jnp.zeros((1, width), jnp.bfloat16)], axis=0
    )[target].astype(jnp.float32)
    grad_gate = kept_value * jnp.sum(grad_out * fetched_value, axis=1)
    grad_logits = ((grad_gate * gate)[:, None] * (route_hot.astype(jnp.float32) - probs)).astype(
        jnp.bfloat16
    )
    grad_router = contract_rows(second_part, grad_logits)
    grad_second = grad_home_rows + contract_cols(grad_logits, full_router)
    lifted_two, grad_gain_two = norm_back(grad_second, unit_two, inverse_two, scale_two)
    grad_middle = grad_out + lifted_two
    grad_branch = grad_middle.astype(jnp.bfloat16)
    grad_proj = contract_rows(grad_branch, mixed_rows)
    grad_mixed = (
        jnp.dot(grad_branch, full_proj, preferred_element_type=jnp.float32)
        .astype(jnp.bfloat16)
        .reshape(slots, local_len, heads, HEAD_DIM)
    )
    delta = jnp.sum(
        grad_mixed.astype(jnp.float32) * blended_layer_yield.astype(jnp.float32), axis=-1
    )
    every_pair = lax.all_gather(pairs, "ctx", axis=1, tiled=True)
    piece_len = every_pair.shape[1]
    key_step_size = math.gcd(piece_len, key_block)

    def inner(number, state):
        grad_query, grad_piece = state
        offset = number * key_step_size
        block = lax.dynamic_slice_in_dim(every_pair, offset, key_step_size, 1)
        keys, values, allowed, scores = score_block(
            query, block, 0 + offset, query_places, lengths, heads
        )
        weights = jnp.where(allowed, jnp.exp(scores - log_total[..., None]), 0.0)
        grad_values = jnp.einsum(
            "sqhk,sqhd->skhd",
            weights.astype(jnp.bfloat16),
            grad_mixed,
            preferred_element_type=jnp.float32,
        )
        grad_weights = jnp.einsum(
            "sqhd,skhd->sqhk", grad_mixed, values, preferred_element_type=jnp.float32
        )
        grad_scores = (weights * (grad_weights - delta[..., None])).astype(jnp.bfloat16)
        grad_query = (
            grad_query
            + jnp.einsum("sqhk,skhd->sqhd", grad_scores, keys, preferred_element_type=jnp.float32)
            * scale
        )
        grad_keys = (
            jnp.einsum("sqhk,sqhd->skhd", grad_scores, query, preferred_element_type=jnp.float32)
            * scale
        )
        update = jnp.concatenate(
            [
                grad_keys.reshape(slots, key_step_size, head_width),
                grad_values.reshape(slots, key_step_size, head_width),
            ],
            axis=-1,
        )
        return (grad_query, lax.dynamic_update_slice_in_dim(grad_piece, update, offset, 1))

    state = (
        jnp.zeros((slots, local_len, heads, HEAD_DIM), jnp.float32),
        jnp.zeros((slots, piece_len, 2 * head_width), jnp.float32),
    )
    grad_query_total, grad_all_pairs = lax.fori_loop(0, piece_len // key_step_size, inner, state)
    grad_pairs = lax.psum_scatter(
        grad_all_pairs.astype(jnp.bfloat16), "ctx", scatter_dimension=1, tiled=True
    )
    grad_query_rows = grad_query_total.astype(jnp.bfloat16).reshape(count, 1, head_width)
    grad_pair_rows = grad_pairs.reshape(count, 2, head_width)
    grad_projected = jnp.concatenate([grad_query_rows, grad_pair_rows], axis=1)
    grad_qkv = jnp.einsum(
        "td,tkf->kdf", first_part, grad_projected, preferred_element_type=jnp.float32
    )
    partial_first = jnp.einsum(
        "tkf,kdf->td", grad_projected, full_qkv, preferred_element_type=jnp.float32
    )
    grad_first = lax.psum(partial_first.astype(jnp.bfloat16), "tp").astype(jnp.float32)
    lifted_one, grad_gain_one = norm_back(grad_first, unit_one, inverse_one, scale_one)
    grad_tokens = (grad_middle + lifted_one).reshape(slots, local_len, width)
    shard_qkv, shard_proj, shard_router, shard_one, shard_two = (
        lax.psum_scatter(grad_qkv, ("shard", "ctx"), scatter_dimension=1, tiled=True),
        lax.psum_scatter(grad_proj, ("shard", "ctx"), scatter_dimension=0, tiled=True),
        lax.psum_scatter(grad_router, ("shard", "ctx"), scatter_dimension=0, tiled=True),
        lax.psum_scatter(grad_gain_one, ("shard", "ctx"), scatter_dimension=0, tiled=True),
        lax.psum_scatter(grad_gain_two, ("shard", "ctx"), scatter_dimension=0, tiled=True),
    )
    return (
        output,
        grad_tokens,
        shard_qkv,
        shard_proj,
        shard_router,
        shard_one,
        shard_two,
        grad_w_in,
        grad_w_out,
    )


def solution(mesh):
    return jax.shard_map(
        local,
        mesh=mesh,
        in_specs=(
            P("shard", "ctx", None),
            P("shard"),
            P("shard", "ctx", None),
            P(None, ("shard", "ctx"), "tp"),
            P(("shard", "ctx"), "tp"),
            P(("shard", "ctx"), None),
            P(("shard", "ctx")),
            P(("shard", "ctx")),
            P(("shard", "ctx"), None, "tp"),
            P(("shard", "ctx"), "tp", None),
            P("shard", "ctx", None),
        ),
        out_specs=(
            P("shard", "ctx", None),
            P("shard", "ctx", None),
            P(None, ("shard", "ctx"), "tp"),
            P(("shard", "ctx"), "tp"),
            P(("shard", "ctx"), None),
            P(("shard", "ctx")),
            P(("shard", "ctx")),
            P(("shard", "ctx"), None, "tp"),
            P(("shard", "ctx"), "tp", None),
        ),
        check_vma=False,
    )
```

profile of v0, /device:TPU:0, one launch (start us, length us, event | category | flops | bytes accessed | tf_op | source)
XLA Modules:
  0.0 1555.6 jit_solution(8912347346169904644)
XLA Ops:
  11.6 43.8 %all-reduce.8 = (bf16[1024]{0:T(1024)(128)(2,1)S(1)}, bf16[1024]{0:T(1024)(128)(2,1)S(1)}) all-reduce(bf16[1024]{0:T(1024)(128)(2,1)S(1)} %dynamic-update-slice.1, bf16[1024]{0:T(1024)(128)(2,1)S(1)} %dynamic-update-slice), channel_id=1, replica_groups=mesh['shard'=4,'ctx'=4,'tp'=2] {'shard','ctx'}, use_global_device_ids=true, to_apply=%add.3 | all-reduce | flops 2048 | bytes 8192
  59.8 21.7 %all-gather.5.cloned.1.call-done = bf16[3,1024,512]{2,1,0:T(8,128)(2,1)} async-done(((bf16[3,64,512]{2,1,0:T(8,128)(2,1)}), bf16[3,1024,512]{2,1,0:T(8,128)(2,1)}) %all-gather.5.cloned.1.call-update) | async-done | bytes 3145744 | tf_op jit(solution)/shard_map/all_gather | solution.py:80
  93.2 83.9 %all-gather.7.cloned.1.call-done = bf16[1,4096,1024]{1,2,0:T(8,128)(2,1)} async-done(((bf16[1,1024,1024]{1,2,0:T(8,128)(2,1)}), bf16[1,4096,1024]{1,2,0:T(8,128)(2,1)}) %all-gather.7.cloned.1.call-update) | async-done | bytes 8388624 | tf_op jit(solution)/shard_map/all_gather | solution.py:101
  177.1 133.8 %while.34 = (s32[]{:T(128)}, f32[1,1024,8]{1,2,0:T(8,128)S(1)}, f32[1,1024,8]{1,2,0:T(8,128)S(1)}, f32[1,1024,8,64]{1,3,2,0:T(8,128)}, s32[1]{0:T(128)}, /*index...) while((s32[]{:T(128)}, f32[1,1024,8]{1,2,0:T(8,128)S(1)}, ...), condition=%wide.region_5.6_spmd.clone, body=%wide.region_2.5_spmd.clone.sunk | while | flops 1130940928 | bytes 61355232 | solution.py:125
  323.7 15.8 %all-reduce.15.cloned.1.call-done = bf16[1024,1024]{1,0:T(8,128)(2,1)} async-done(((bf16[1024,1024]{1,0:T(8,128)(2,1)}), bf16[1024,1024]{1,0:T(8,128)(2,1)}) %all-reduce.15.cloned.1.call-update) | async-done | bytes 2097168 | tf_op jit(solution)/shard_map/psum | solution.py:132
  363.6 78.6 %all-gather = bf16[16,64,16]{1,2,0:T(8,128)(2,1)S(1)} all-gather(bf16[1,64,16]{1,2,0:T(8,128)(2,1)S(1)} %bitcast.394), channel_id=1, replica_groups=mesh['shard'=4,'ctx'=4,'tp'=2] {'shard','ctx'}, dimensions={0}, use_global_device_ids=true | all-gather | bytes 34816 | tf_op jit(solution)/shard_map/all_gather | solution.py:82
  456.3 10.4 all-to-all-start.2
  487.0 26.5 %all-to-all-done.2 = bf16[16,80,1024]{2,1,0:T(8,128)(2,1)} async-done(((bf16[16,80,1024]{2,1,0:T(8,128)(2,1)}), bf16[16,80,1024]{2,1,0:T(8,128)(2,1)}, u32[]{:S(2)}, u32[]{:S(2)}) %all-to-all-start.2) | async-done | bytes 2621472 | tf_op jit(solution)/shard_map/all_to_all | solution.py:190
  513.5 15.5 fusion.50
  536.3 35.1 %all-reduce.21.cloned.1.call-done = (bf16[16,80,1024]{2,1,0:T(8,128)(2,1)}, bf16[16,80,1024]{2,1,0:T(8,128)(2,1)}) async-done(((bf16[16,80,1024]{2,1,0:T(8,128)(2,1)}, bf16[16,80,1024]{2,1,0:T(8,128)(2,1)}), (bf16[16,80,1024]{2,1,0:T(8,128)(2,1)}, bf16[16,80,1024]{2,1,0:T(8,128)(2,1)})) %all-reduce.21.cloned.1.call-update) | async-done | bytes 5242896 | tf_op jit(solution)/shard_map/psum | solution.py:160
  571.4 67.3 %all_to_all.20 = bf16[16,80,1024]{2,1,0:T(8,128)(2,1)} all-to-all(bf16[16,80,1024]{2,1,0:T(8,128)(2,1)} %get-tuple-element.465), channel_id=1, replica_groups=mesh['shard'=4,'ctx'=4,'tp'=2] {'shard','ctx'}, dimensions={0} | all-to-all | bytes 5242880 | tf_op jit(solution)/shard_map/all_to_all | solution.py:204
  654.8 39.5 %all-to-all-done.1 = bf16[16,80,1024]{2,1,0:T(8,128)(2,1)} async-done(((bf16[16,80,1024]{2,1,0:T(8,128)(2,1)}), bf16[16,80,1024]{2,1,0:T(8,128)(2,1)}, u32[]{:S(2)}, u32[]{:S(2)}) %all-to-all-start.1) | async-done | bytes 2621472 | tf_op jit(solution)/shard_map/all_to_all | solution.py:161
  724.1 284.5 %while.35 = (s32[]{:T(128)}, f32[1,1024,8,64]{1,3,2,0:T(8,128)}, bf16[1,4096,1024]{1,2,0:T(8,128)(2,1)}, bf16[1,4096,1024]{1,2,0:T(8,128)(2,1)}, s32[1]{0:T(128)...) while((s32[]{:T(128)}, f32[1,1024,8,64]{1,3,2,0:T(8,128)}, ...), condition=%wide.region_24.25_spmd.clone, body=%wide.region_23.24_spmd.clone.sunk | while | flops 2731543040 | bytes 109163824 | solution.py:276
  779.8 9.5 fusion.179
  815.3 9.5 fusion.179
  850.8 9.5 fusion.179
  1015.4 86.0 %reduce-scatter.6.cloned.1.call-done = bf16[1,1024,1024]{1,2,0:T(8,128)(2,1)} async-done(((bf16[1,4096,1024]{1,2,0:T(8,128)(2,1)}), bf16[1,1024,1024]{1,2,0:T(8,128)(2,1)}) %reduce-scatter.6.cloned.1.call-update) | async-done | bytes 2097168 | tf_op jit(solution)/shard_map/reduce_scatter | solution.py:277
  1136.5 11.0 convolution_bitcast_fusion.1
  1147.5 12.3 convolution_bitcast_fusion
  1159.8 21.4 %reduce-scatter.10.cloned.1.call-done = f32[64,16]{1,0:T(8,128)} async-done(((f32[1024,16]{1,0:T(8,128)}), f32[64,16]{1,0:T(8,128)}) %reduce-scatter.10.cloned.1.call-update) | async-done | bytes 4112
  1182.6 18.6 %all-reduce.17.cloned.1.call-done = bf16[1024,1024]{1,0:T(8,128)(2,1)} async-done(((bf16[1024,1024]{1,0:T(8,128)(2,1)}), bf16[1024,1024]{1,0:T(8,128)(2,1)}) %all-reduce.17.cloned.1.call-update) | async-done | bytes 2097168 | tf_op jit(solution)/shard_map/psum | solution.py:289
  1204.7 44.8 %all-reduce.7 = (f32[1024]{0:T(1024)S(1)}, f32[1024]{0:T(1024)S(1)}) all-reduce(f32[1024]{0:T(1024)S(1)} %get-tuple-element.420, f32[1024]{0:T(1024)S(1)} %copy-done.33), channel_id=6, replica_groups=mesh['shard'=4,'ctx'=4,'tp'=2] {'shard','ctx'}, use_global_device_ids=true, to_apply=%region_33.34.clone | all-reduce | flops 2048 | bytes 16384
  1255.7 209.6 %all-reduce.19.cloned.1.call-done = f32[3,1024,512]{2,0,1:T(4,128)} async-done(((f32[3,1024,512]{2,0,1:T(4,128)}), f32[3,1024,512]{2,0,1:T(4,128)}) %all-reduce.19.cloned.1.call-update) | async-done | bytes 6291472
  1467.3 81.3 %reduce-scatter.8.cloned.1.call-done = f32[64,512]{1,0:T(8,128)} async-done(((f32[1024,512]{1,0:T(8,128)}), f32[64,512]{1,0:T(8,128)}) %reduce-scatter.8.cloned.1.call-update) | async-done | bytes 131088 | tf_op jit(solution)/shard_map/reduce_scatter | solution.py:294
  (385 shorter events, 585.3 us)
Async XLA Ops:
  7.2 74.3 %copy-start = (bf16[1,1024,1024]{2,1,0:T(8,128)(2,1)S(1)}, bf16[1,1024,1024]{2,1,0:T(8,128)(2,1)}, u32[]{:S(2)}) copy-start(bf16[1,1024,1024]{2,1,0:T(8,128)(2,1)} %param.15) | copy-start | bytes 6291460
  7.2 74.3 %all-gather.5.cloned.1.call-start = ((), (), s32[]{:S(2)}) async-start(), calls=%async_computation.7 | async-start | bytes 3342336 | tf_op jit(solution)/shard_map/all_gather | solution.py:80
  7.9 169.2 %all-gather.7.cloned.1.call-start = ((), (), s32[]{:S(2)}) async-start(), calls=%async_computation.8 | async-start | bytes 10485760 | tf_op jit(solution)/shard_map/all_gather | solution.py:101
  55.5 32.1 %copy-start.26 = (f32[1024]{0:T(1024)}, f32[1024]{0:T(1024)S(1)}, u32[]{:S(2)}) copy-start(f32[1024]{0:T(1024)S(1)} %convert_element_type.129) | copy-start | bytes 12292
  57.5 30.2 %copy-start.22 = (f32[1024]{0:T(1024)}, f32[1024]{0:T(1024)S(1)}, u32[]{:S(2)}) copy-start(f32[1024]{0:T(1024)S(1)} %broadcast_multiply_fusion.5) | copy-start | bytes 12292
  59.8 27.9 %copy-start.28 = (f32[1024]{0:T(1024)}, f32[1024]{0:T(1024)S(1)}, u32[]{:S(2)}) copy-start(f32[1024]{0:T(1024)S(1)} %add_rsqrt_fusion.1) | copy-start | bytes 12292
  90.8 222.9 %all-gather.9.cloned.1.call-start = ((), (), s32[]{:S(2)}) async-start(), calls=%async_computation.9 | async-start | bytes 1114112 | tf_op jit(solution)/shard_map/all_gather | solution.py:81
  91.6 247.8 %all-reduce.15.cloned.1.call-start = ((), (), s32[]{:S(2)}) async-start(), calls=%async_computation.10 | async-start | bytes 4194304 | tf_op jit(solution)/shard_map/psum | solution.py:132
  356.7 99.6 %all-to-all-start = ((bf16[16,80,1024]{2,1,0:T(8,128)(2,1)}), bf16[16,80,1024]{2,1,0:T(8,128)(2,1)}, u32[]{:S(2)}, u32[]{:S(2)}) async-start(bf16[16,80,1024]{2,1,0:T(8,128)(2,1)} %bitcast.365), calls=%async_computation | async-start | bytes 5242880 | tf_op jit(solution)/shard_map/all_to_all | solution.py:154
  444.6 264.5 %copy-start.16 = (f32[1024,16]{0,1:T(8,128)}, f32[1024,16]{0,1:T(8,128)S(1)}, u32[]{:S(2)}) copy-start(f32[1024,16]{0,1:T(8,128)S(1)} %get-tuple-element.481) | copy-start | bytes 196612
  444.6 264.5 %copy-start.20 = (f32[1024]{0:T(1024)}, f32[1024]{0:T(1024)S(1)}, u32[]{:S(2)}) copy-start(f32[1024]{0:T(1024)S(1)} %get-tuple-element.480) | copy-start | bytes 12292
  444.7 264.5 %copy-start.24 = (f32[1024]{0:T(1024)}, f32[1024]{0:T(1024)S(1)}, u32[]{:S(2)}) copy-start(f32[1024]{0:T(1024)S(1)} %fusion.112) | copy-start | bytes 12292
  456.3 57.2 %all-to-all-start.2 = ((bf16[16,80,1024]{2,1,0:T(8,128)(2,1)}), bf16[16,80,1024]{2,1,0:T(8,128)(2,1)}, u32[]{:S(2)}, u32[]{:S(2)}) async-start(bf16[16,80,1024]{2,1,0:T(8,128)(2,1)} %bitcast.367), calls=%async_computation.2 | async-start | bytes 5242880 | tf_op jit(solution)/shard_map/all_to_all | solution.py:190
  466.7 104.7 %all-reduce.21.cloned.1.call-start = ((), (), s32[]{:S(2)}) async-start(), calls=%async_computation.16 | async-start | bytes 10485760 | tf_op jit(solution)/shard_map/psum | solution.py:160
  466.7 12.6 copy-start.34
  513.5 15.5 copy-start.35
  638.7 55.6 %all-to-all-start.1 = ((bf16[16,80,1024]{2,1,0:T(8,128)(2,1)}), bf16[16,80,1024]{2,1,0:T(8,128)(2,1)}, u32[]{:S(2)}, u32[]{:S(2)}) async-start(bf16[16,80,1024]{2,1,0:T(8,128)(2,1)} %get-tuple-element.464), calls=%async_computation.1 | async-start | bytes 5242880 | tf_op jit(solution)/shard_map/all_to_all | solution.py:161
  643.2 458.2 %reduce-scatter.6.cloned.1.call-start = ((), (), s32[]{:S(2)}) async-start(), calls=%async_computation.11 | async-start | bytes 10485760 | tf_op jit(solution)/shard_map/reduce_scatter | solution.py:277
  1008.6 172.6 %reduce-scatter.10.cloned.1.call-start = ((), (), s32[]{:S(2)}) async-start(), calls=%async_computation.14 | async-start | bytes 557056
  1011.9 93.5 %copy-start.15 = (bf16[1024,1,512]{2,0,1:T(8,128)(2,1)S(1)}, bf16[1024,1,512]{2,0,1:T(8,128)(2,1)}, u32[]{:S(2)}) copy-start(bf16[1024,1,512]{2,0,1:T(8,128)(2,1)} %copy.50) | copy-start | bytes 3145732
  1015.3 185.9 %all-reduce.17.cloned.1.call-start = ((), (), s32[]{:S(2)}) async-start(), calls=%async_computation.12 | async-start | bytes 4194304 | tf_op jit(solution)/shard_map/psum | solution.py:289
  1112.8 352.4 %all-reduce.19.cloned.1.call-start = ((), (), s32[]{:S(2)}) async-start(), calls=%async_computation.15 | async-start | bytes 16777216
  1130.4 418.2 %reduce-scatter.8.cloned.1.call-start = ((), (), s32[]{:S(2)}) async-start(), calls=%async_computation.13 | async-start | bytes 2228224 | tf_op jit(solution)/shard_map/reduce_scatter | solution.py:294
  1159.8 44.9 %copy-start.33 = (f32[1024]{0:T(1024)S(1)}, f32[1024]{0:T(1024)}, u32[]{:S(2)}) copy-start(f32[1024]{0:T(1024)} %get-tuple-element.418) | copy-start | bytes 12292
  (42 other events, 142.1 us)
Sparse Core Ops, SparseCore 0:
  10.8 70.7 all-gather.4
  91.0 86.0 all-gather.6
  179.9 55.1 all-gather.8
  318.1 21.2 all-reduce.14
  536.4 34.9 all-reduce.20
  1008.7 92.6 reduce-scatter.5
  1103.7 77.4 reduce-scatter.9
  1183.6 17.6 all-reduce.16
  1207.3 257.9 all-reduce.18
  1468.0 80.5 reduce-scatter.7
where the time goes:
time: 1560 us
  waiting for transfers between devices  641 us (41%)
  matrix products  435 us (28%)
  blocking collectives  235 us (15%)
  local copies, waits for them, and re-layouts  103 us (7%)
  other arithmetic  100 us (6%)
  starting transfers between devices  22.4 us (1%)
  between operations  17.1 us (1%)
    unnamed x12, waiting for transfers between devices  232 us
    unnamed x2, blocking collectives  88.6 us
    dot_general x16, matrix products, score_block(): jnp.einsum('sqhd,skhd->sqhk', query, keys, preferred_element_type=jnp.flo...  87 us
    reduce_scatter x1, waiting for transfers between devices, local(): lax.psum_scatter(grad_all_pairs.astype(jnp.bfloat16), 'ctx', scatter_dime...  86 us
    all_gather x1, waiting for transfers between devices, local(): piece = lax.all_gather(pairs, 'ctx', axis=1, tiled=True)  83.9 us
    reduce_scatter x1, waiting for transfers between devices, local(): lax.psum_scatter(grad_proj, ('shard', 'ctx'), scatter_dimension=0, tiled=...  81.3 us
    all_gather x1, blocking collectives, local(): lax.all_gather(router, ('shard', 'ctx'), axis=0, tiled=True)  78.6 us
    dot_general x8, matrix products, inner(): jnp.einsum('sqhd,skhd->sqhk', grad_mixed, values, preferred_element_type=...  75.8 us
  transfers between devices with their start and end apart: 13, of which 11 were waited for; matrix products, arithmetic and copies ran while one was open for 17% of the time, Pallas kernels for 0%

commit v1 on v0

--- a/solution.py
+++ b/solution.py
@@ -158,13 +158,20 @@
     hidden = jax.nn.gelu(pre).astype(jnp.bfloat16)
     partial_out = jnp.dot(hidden, w_out[0], preferred_element_type=jnp.float32)
     summed = lax.psum(partial_out.astype(jnp.bfloat16), "tp")
-    going_back = lax.all_to_all(
-        summed.reshape(sources, items, width),
-        ("shard", "ctx"),
-        split_axis=0,
-        concat_axis=0,
-        tiled=True,
-    )
+    x = summed.reshape(sources, items, width)
+    ways, here = (lax.axis_size(("shard", "ctx")), lax.axis_index(("shard", "ctx")))
+    width_2 = x.shape[0] // ways
+    shape = list(x.shape)
+    shape[0] = width_2
+    height = shape[0]
+    shape[0] = height * ways
+    full = jnp.zeros(shape, x.dtype)
+    for mask in range(ways):
+        part = lax.dynamic_slice_in_dim(x, (here ^ mask) * width_2, width_2, axis=0)
+        if mask:
+            part = lax.ppermute(part, ("shard", "ctx"), [(d, d ^ mask) for d in range(ways)])
+        full = lax.dynamic_update_slice_in_dim(full, part, (here ^ mask) * height, axis=0)
+    going_back = full
     pre_act = pre.reshape(sources, items, pre.shape[1])
     fetched = jnp.concatenate(
         [going_back.reshape(experts * capacity, width), jnp.zeros((1, width), jnp.bfloat16)], axis=0

time: 1560 us -> 1570 us (level)
  blocking collectives: 235 us -> 167 us
  starting transfers between devices: 22.4 us -> 71.4 us
  waiting for transfers between devices: 641 us -> 667 us
    ppermute x0 -> x15, waiting for transfers between devices: none -> 73.6 us  [local(): lax.ppermute(part, ('shard', 'ctx'), [(d, d ^ mask) for d in range(ways)])]
    all_to_all x1 -> x0, blocking collectives: 67.3 us -> none  [local(): lax.all_to_all(grad_dispatched.reshape(arrived_here.shape), ('shard', 'ct...]
    ppermute x0 -> x15, starting transfers between devices: none -> 46.3 us  [local(): lax.ppermute(part, ('shard', 'ctx'), [(d, d ^ mask) for d in range(ways)])]
    all_to_all x1, waiting for transfers between devices: 39.5 us -> 0.01 us  [local(): lax.all_to_all(grad_dispatched.reshape(arrived_here.shape), ('shard', 'ct...]
  transfers between devices with their start and end apart: 13 -> 28, of which waited for: 11 -> 18; matrix products, arithmetic and copies ran while one was open for 17% -> 17% of each run, Pallas kernels for 0% -> 0%
where the time goes in v1:
time: 1570 us; the launch traced here: 1560 us
  waiting for transfers between devices  667 us (42%)
  matrix products  438 us (28%)
  blocking collectives  167 us (11%)
  local copies, waits for them, and re-layouts  102 us (6%)
  other arithmetic  100 us (6%)
  starting transfers between devices  71.4 us (5%)
  between operations  17.3 us (1%)
    unnamed x12, waiting for transfers between devices  233 us
    unnamed x2, blocking collectives  88.6 us
    dot_general x16, matrix products, score_block(): jnp.einsum('sqhd,skhd->sqhk', query, keys, preferred_element_type=jnp.flo...  87.2 us
    all_gather x1, waiting for transfers between devices, local(): piece = lax.all_gather(pairs, 'ctx', axis=1, tiled=True)  83.8 us
    reduce_scatter x1, waiting for transfers between devices, local(): lax.psum_scatter(grad_proj, ('shard', 'ctx'), scatter_dimension=0, tiled=...  81.3 us
    all_gather x1, blocking collectives, local(): lax.all_gather(router, ('shard', 'ctx'), axis=0, tiled=True)  78.6 us
    reduce_scatter x1, waiting for transfers between devices, local(): lax.psum_scatter(grad_all_pairs.astype(jnp.bfloat16), 'ctx', scatter_dime...  77.8 us
    dot_general x8, matrix products, inner(): jnp.einsum('sqhd,skhd->sqhk', grad_mixed, values, preferred_element_type=...  75.7 us
  transfers between devices with their start and end apart: 28, of which 18 were waited for; matrix products, arithmetic and copies ran while one was open for 17% of the time, Pallas kernels for 0%

profile of v1, /device:TPU:0, one launch (start us, length us, event | category | flops | bytes accessed | tf_op | source)
XLA Modules:
  0.0 1564.6 jit_solution(14631718573106760288)
XLA Ops:
  11.6 43.8 %all-reduce.8 = (bf16[1024]{0:T(1024)(128)(2,1)S(1)}, bf16[1024]{0:T(1024)(128)(2,1)S(1)}) all-reduce(bf16[1024]{0:T(1024)(128)(2,1)S(1)} %dynamic-update-slice.1, bf16[1024]{0:T(1024)(128)(2,1)S(1)} %dynamic-update-slice), channel_id=1, replica_groups=mesh['shard'=4,'ctx'=4,'tp'=2] {'shard','ctx'}, use_global_device_ids=true, to_apply=%add.3 | all-reduce | flops 2048 | bytes 8192
  59.8 21.7 %all-gather.5.cloned.1.call-done = bf16[3,1024,512]{2,1,0:T(8,128)(2,1)} async-done(((bf16[3,64,512]{2,1,0:T(8,128)(2,1)}), bf16[3,1024,512]{2,1,0:T(8,128)(2,1)}) %all-gather.5.cloned.1.call-update) | async-done | bytes 3145744 | tf_op jit(solution)/shard_map/all_gather | solution.py:80
  93.2 83.8 %all-gather.7.cloned.1.call-done = bf16[1,4096,1024]{1,2,0:T(8,128)(2,1)} async-done(((bf16[1,1024,1024]{1,2,0:T(8,128)(2,1)}), bf16[1,4096,1024]{1,2,0:T(8,128)(2,1)}) %all-gather.7.cloned.1.call-update) | async-done | bytes 8388624 | tf_op jit(solution)/shard_map/all_gather | solution.py:101
  177.1 133.9 %while.34 = (s32[]{:T(128)}, f32[1,1024,8]{1,2,0:T(8,128)S(1)}, f32[1,1024,8]{1,2,0:T(8,128)S(1)}, f32[1,1024,8,64]{1,3,2,0:T(8,128)}, s32[1]{0:T(128)}, /*index...) while((s32[]{:T(128)}, f32[1,1024,8]{1,2,0:T(8,128)S(1)}, ...), condition=%wide.region_5.6_spmd.clone, body=%wide.region_2.5_spmd.clone.sunk | while | flops 1130940928 | bytes 61355232 | solution.py:125
  323.8 15.8 %all-reduce.15.cloned.1.call-done = bf16[1024,1024]{1,0:T(8,128)(2,1)} async-done(((bf16[1024,1024]{1,0:T(8,128)(2,1)}), bf16[1024,1024]{1,0:T(8,128)(2,1)}) %all-reduce.15.cloned.1.call-update) | async-done | bytes 2097168 | tf_op jit(solution)/shard_map/psum | solution.py:132
  363.7 78.6 %all-gather = bf16[16,64,16]{1,2,0:T(8,128)(2,1)S(1)} all-gather(bf16[1,64,16]{1,2,0:T(8,128)(2,1)S(1)} %bitcast.394), channel_id=1, replica_groups=mesh['shard'=4,'ctx'=4,'tp'=2] {'shard','ctx'}, dimensions={0}, use_global_device_ids=true | all-gather | bytes 34816 | tf_op jit(solution)/shard_map/all_gather | solution.py:82
  456.4 10.4 all-to-all-start.1
  487.1 26.5 %all-to-all-done.1 = bf16[16,80,1024]{2,1,0:T(8,128)(2,1)} async-done(((bf16[16,80,1024]{2,1,0:T(8,128)(2,1)}), bf16[16,80,1024]{2,1,0:T(8,128)(2,1)}, u32[]{:S(2)}, u32[]{:S(2)}) %all-to-all-start.1) | async-done | bytes 2621472 | tf_op jit(solution)/shard_map/all_to_all | solution.py:197
  513.6 15.5 fusion.50
  536.4 35.1 %all-reduce.21.cloned.1.call-done = (bf16[16,80,1024]{2,1,0:T(8,128)(2,1)}, bf16[16,80,1024]{2,1,0:T(8,128)(2,1)}) async-done(((bf16[16,80,1024]{2,1,0:T(8,128)(2,1)}, bf16[16,80,1024]{2,1,0:T(8,128)(2,1)}), (bf16[16,80,1024]{2,1,0:T(8,128)(2,1)}, bf16[16,80,1024]{2,1,0:T(8,128)(2,1)})) %all-reduce.21.cloned.1.call-update) | async-done | bytes 5242896 | tf_op jit(solution)/shard_map/psum | solution.py:160
  594.0 14.5 collective-permute-done.1
  611.3 26.3 %collective-permute-done.3 = bf16[1,80,1024]{2,1,0:T(8,128)(2,1)S(1)} collective-permute-done((bf16[1,80,1024]{2,1,0:T(8,128)(2,1)S(1)}, bf16[1,80,1024]{2,1,0:T(8,128)(2,1)S(1)}, u32[]{:S(2)}, u32[]{:S(2)}) %collective-permute-start.3) | collective-permute-done | bytes 163872 | tf_op jit(solution)/shard_map/ppermute | solution.py:172
  660.0 14.5 collective-permute-done.7
  742.3 284.7 %while.35 = (s32[]{:T(128)}, f32[1,1024,8,64]{1,3,2,0:T(8,128)}, bf16[1,4096,1024]{1,2,0:T(8,128)(2,1)}, bf16[1,4096,1024]{1,2,0:T(8,128)(2,1)}, s32[1]{0:T(128)...) while((s32[]{:T(128)}, f32[1,1024,8,64]{1,3,2,0:T(8,128)}, ...), condition=%wide.region_24.25_spmd.clone, body=%wide.region_23.24_spmd.clone.sunk | while | flops 2731543040 | bytes 109163824 | solution.py:283
  762.5 9.5 fusion.179
  869.1 9.5 fusion.179
  1032.7 77.8 %reduce-scatter.6.cloned.1.call-done = bf16[1,1024,1024]{1,2,0:T(8,128)(2,1)} async-done(((bf16[1,4096,1024]{1,2,0:T(8,128)(2,1)}), bf16[1,1024,1024]{1,2,0:T(8,128)(2,1)}) %reduce-scatter.6.cloned.1.call-update) | async-done | bytes 2097168 | tf_op jit(solution)/shard_map/reduce_scatter | solution.py:284
  1145.6 10.8 convolution_bitcast_fusion.1
  1156.4 12.3 convolution_bitcast_fusion
  1168.7 21.6 %reduce-scatter.10.cloned.1.call-done = f32[64,16]{1,0:T(8,128)} async-done(((f32[1024,16]{1,0:T(8,128)}), f32[64,16]{1,0:T(8,128)}) %reduce-scatter.10.cloned.1.call-update) | async-done | bytes 4112
  1191.7 18.6 %all-reduce.17.cloned.1.call-done = bf16[1024,1024]{1,0:T(8,128)(2,1)} async-done(((bf16[1024,1024]{1,0:T(8,128)(2,1)}), bf16[1024,1024]{1,0:T(8,128)(2,1)}) %all-reduce.17.cloned.1.call-update) | async-done | bytes 2097168 | tf_op jit(solution)/shard_map/psum | solution.py:296
  1213.7 44.8 %all-reduce.7 = (f32[1024]{0:T(1024)S(1)}, f32[1024]{0:T(1024)S(1)}) all-reduce(f32[1024]{0:T(1024)S(1)} %get-tuple-element.420, f32[1024]{0:T(1024)S(1)} %copy-done.33), channel_id=6, replica_groups=mesh['shard'=4,'ctx'=4,'tp'=2] {'shard','ctx'}, use_global_device_ids=true, to_apply=%region_33.34.clone | all-reduce | flops 2048 | bytes 16384
  1264.7 209.6 %all-reduce.19.cloned.1.call-done = f32[3,1024,512]{2,0,1:T(4,128)} async-done(((f32[3,1024,512]{2,0,1:T(4,128)}), f32[3,1024,512]{2,0,1:T(4,128)}) %all-reduce.19.cloned.1.call-update) | async-done | bytes 6291472
  1476.3 81.3 %reduce-scatter.8.cloned.1.call-done = f32[64,512]{1,0:T(8,128)} async-done(((f32[1024,512]{1,0:T(8,128)}), f32[64,512]{1,0:T(8,128)}) %reduce-scatter.8.cloned.1.call-update) | async-done | bytes 131088 | tf_op jit(solution)/shard_map/reduce_scatter | solution.py:301
  (431 shorter events, 663.4 us)
Async XLA Ops:
  7.2 74.3 %all-gather.5.cloned.1.call-start = ((), (), s32[]{:S(2)}) async-start(), calls=%async_computation.6 | async-start | bytes 3342336 | tf_op jit(solution)/shard_map/all_gather | solution.py:80
  7.9 169.2 %all-gather.7.cloned.1.call-start = ((), (), s32[]{:S(2)}) async-start(), calls=%async_computation.7 | async-start | bytes 10485760 | tf_op jit(solution)/shard_map/all_gather | solution.py:101
  90.8 223.0 %all-gather.9.cloned.1.call-start = ((), (), s32[]{:S(2)}) async-start(), calls=%async_computation.8 | async-start | bytes 1114112 | tf_op jit(solution)/shard_map/all_gather | solution.py:81
  91.6 248.0 %all-reduce.15.cloned.1.call-start = ((), (), s32[]{:S(2)}) async-start(), calls=%async_computation.9 | async-start | bytes 4194304 | tf_op jit(solution)/shard_map/psum | solution.py:132
  356.8 99.6 %all-to-all-start = ((bf16[16,80,1024]{2,1,0:T(8,128)(2,1)}), bf16[16,80,1024]{2,1,0:T(8,128)(2,1)}, u32[]{:S(2)}, u32[]{:S(2)}) async-start(bf16[16,80,1024]{2,1,0:T(8,128)(2,1)} %bitcast.365), calls=%async_computation | async-start | bytes 5242880 | tf_op jit(solution)/shard_map/all_to_all | solution.py:154
  456.4 57.2 %all-to-all-start.1 = ((bf16[16,80,1024]{2,1,0:T(8,128)(2,1)}), bf16[16,80,1024]{2,1,0:T(8,128)(2,1)}, u32[]{:S(2)}, u32[]{:S(2)}) async-start(bf16[16,80,1024]{2,1,0:T(8,128)(2,1)} %bitcast.367), calls=%async_computation.1 | async-start | bytes 5242880 | tf_op jit(solution)/shard_map/all_to_all | solution.py:197
  466.8 104.7 %all-reduce.21.cloned.1.call-start = ((), (), s32[]{:S(2)}) async-start(), calls=%async_computation.15 | async-start | bytes 10485760 | tf_op jit(solution)/shard_map/psum | solution.py:160
  571.5 142.3 %all-to-all-start.2 = ((bf16[16,80,1024]{2,1,0:T(8,128)(2,1)}), bf16[16,80,1024]{2,1,0:T(8,128)(2,1)}, u32[]{:S(2)}, u32[]{:S(2)}) async-start(bf16[16,80,1024]{2,1,0:T(8,128)(2,1)} %get-tuple-element.465), calls=%async_computation.2 | async-start | bytes 5242880 | tf_op jit(solution)/shard_map/all_to_all | solution.py:211
  578.4 532.1 %reduce-scatter.6.cloned.1.call-start = ((), (), s32[]{:S(2)}) async-start(), calls=%async_computation.10 | async-start | bytes 10485760 | tf_op jit(solution)/shard_map/reduce_scatter | solution.py:284
  580.7 27.8 %collective-permute-start.1 = (bf16[1,80,1024]{2,1,0:T(8,128)(2,1)S(1)}, bf16[1,80,1024]{2,1,0:T(8,128)(2,1)S(1)}, u32[]{:S(2)}, u32[]{:S(2)}) collective-permute-start(bf16[1,80,1024]{2,1,0:T(8,128)(2,1)S(1)} %get-tuple-element.491), channel_id=1, source_target_pairs={{0,4},{2,6},{4,0},{6,2},{8,12},{10,14},{12,8},{14,10},{16,20},{18,... | collective-permute-start | bytes 491528 | tf_op jit(solution)/shard_map/ppermute | solution.py:172
  584.1 116.8 %collective-permute-start.14 = (bf16[1,80,1024]{2,1,0:T(8,128)(2,1)S(1)}, bf16[1,80,1024]{2,1,0:T(8,128)(2,1)S(1)}, u32[]{:S(2)}, u32[]{:S(2)}) collective-permute-start(bf16[1,80,1024]{2,1,0:T(8,128)(2,1)S(1)} %get-tuple-element.478), channel_id=1, source_target_pairs={{0,30},{2,28},{4,26},{6,24},{8,22},{10,20},{12,18},{14,16},{16,14}... | collective-permute-start | bytes 491528 | tf_op jit(solution)/shard_map/ppermute | solution.py:172
  587.4 113.4 %collective-permute-start.13 = (bf16[1,80,1024]{2,1,0:T(8,128)(2,1)S(1)}, bf16[1,80,1024]{2,1,0:T(8,128)(2,1)S(1)}, u32[]{:S(2)}, u32[]{:S(2)}) collective-permute-start(bf16[1,80,1024]{2,1,0:T(8,128)(2,1)S(1)} %get-tuple-element.479), channel_id=1, source_target_pairs={{0,28},{2,30},{4,24},{6,26},{8,20},{10,22},{12,16},{14,18},{16,12}... | collective-permute-start | bytes 491528 | tf_op jit(solution)/shard_map/ppermute | solution.py:172
  588.9 111.9 %collective-permute-start.12 = (bf16[1,80,1024]{2,1,0:T(8,128)(2,1)S(1)}, bf16[1,80,1024]{2,1,0:T(8,128)(2,1)S(1)}, u32[]{:S(2)}, u32[]{:S(2)}) collective-permute-start(bf16[1,80,1024]{2,1,0:T(8,128)(2,1)S(1)} %get-tuple-element.480), channel_id=1, source_target_pairs={{0,26},{2,24},{4,30},{6,28},{8,18},{10,16},{12,22},{14,20},{16,10}... | collective-permute-start | bytes 491528 | tf_op jit(solution)/shard_map/ppermute | solution.py:172
  593.0 15.5 collective-permute-start.2
  608.5 29.1 %collective-permute-start.3 = (bf16[1,80,1024]{2,1,0:T(8,128)(2,1)S(1)}, bf16[1,80,1024]{2,1,0:T(8,128)(2,1)S(1)}, u32[]{:S(2)}, u32[]{:S(2)}) collective-permute-start(bf16[1,80,1024]{2,1,0:T(8,128)(2,1)S(1)} %get-tuple-element.489), channel_id=1, source_target_pairs={{0,8},{2,10},{4,12},{6,14},{8,0},{10,2},{12,4},{14,6},{16,24},{18,... | collective-permute-start | bytes 491528 | tf_op jit(solution)/shard_map/ppermute | solution.py:172
  608.5 33.6 %collective-permute-start.4 = (bf16[1,80,1024]{2,1,0:T(8,128)(2,1)S(1)}, bf16[1,80,1024]{2,1,0:T(8,128)(2,1)S(1)}, u32[]{:S(2)}, u32[]{:S(2)}) collective-permute-start(bf16[1,80,1024]{2,1,0:T(8,128)(2,1)S(1)} %get-tuple-element.488), channel_id=1, source_target_pairs={{0,10},{2,8},{4,14},{6,12},{8,2},{10,0},{12,6},{14,4},{16,26},{18,... | collective-permute-start | bytes 491528 | tf_op jit(solution)/shard_map/ppermute | solution.py:172
  648.8 25.7 %collective-permute-start.7 = (bf16[1,80,1024]{2,1,0:T(8,128)(2,1)S(1)}, bf16[1,80,1024]{2,1,0:T(8,128)(2,1)S(1)}, u32[]{:S(2)}, u32[]{:S(2)}) collective-permute-start(bf16[1,80,1024]{2,1,0:T(8,128)(2,1)S(1)} %get-tuple-element.485), channel_id=1, source_target_pairs={{0,16},{2,18},{4,20},{6,22},{8,24},{10,26},{12,28},{14,30},{16,0},... | collective-permute-start | bytes 491528 | tf_op jit(solution)/shard_map/ppermute | solution.py:172
  654.5 31.1 %collective-permute-start.8 = (bf16[1,80,1024]{2,1,0:T(8,128)(2,1)S(1)}, bf16[1,80,1024]{2,1,0:T(8,128)(2,1)S(1)}, u32[]{:S(2)}, u32[]{:S(2)}) collective-permute-start(bf16[1,80,1024]{2,1,0:T(8,128)(2,1)S(1)} %get-tuple-element.484), channel_id=1, source_target_pairs={{0,18},{2,16},{4,22},{6,20},{8,26},{10,24},{12,30},{14,28},{16,2},... | collective-permute-start | bytes 491528 | tf_op jit(solution)/shard_map/ppermute | solution.py:172
  674.5 19.1 %collective-permute-start.9 = (bf16[1,80,1024]{2,1,0:T(8,128)(2,1)S(1)}, bf16[1,80,1024]{2,1,0:T(8,128)(2,1)S(1)}, u32[]{:S(2)}, u32[]{:S(2)}) collective-permute-start(bf16[1,80,1024]{2,1,0:T(8,128)(2,1)S(1)} %get-tuple-element.483), channel_id=1, source_target_pairs={{0,20},{2,22},{4,16},{6,18},{8,28},{10,30},{12,24},{14,26},{16,4},... | collective-permute-start | bytes 491528 | tf_op jit(solution)/shard_map/ppermute | solution.py:172
  685.5 13.3 collective-permute-start.10
  1027.0 163.2 %reduce-scatter.10.cloned.1.call-start = ((), (), s32[]{:S(2)}) async-start(), calls=%async_computation.13 | async-start | bytes 557056
  1031.2 179.1 %all-reduce.17.cloned.1.call-start = ((), (), s32[]{:S(2)}) async-start(), calls=%async_computation.11 | async-start | bytes 4194304 | tf_op jit(solution)/shard_map/psum | solution.py:296
  1121.9 352.4 %all-reduce.19.cloned.1.call-start = ((), (), s32[]{:S(2)}) async-start(), calls=%async_computation.14 | async-start | bytes 16777216
  1139.5 418.1 %reduce-scatter.8.cloned.1.call-start = ((), (), s32[]{:S(2)}) async-start(), calls=%async_computation.12 | async-start | bytes 2228224 | tf_op jit(solution)/shard_map/reduce_scatter | solution.py:301
  (57 other events, 1348.2 us)
Sparse Core Ops, SparseCore 0:
  10.8 70.7 all-gather.4
  91.0 86.0 all-gather.6
  179.9 55.1 all-gather.8
  318.2 21.2 all-reduce.14
  536.5 34.9 all-reduce.20
  1027.1 83.2 reduce-scatter.5
  1112.7 77.4 reduce-scatter.9
  1192.6 17.6 all-reduce.16
  1216.3 257.9 all-reduce.18
  1477.0 80.5 reduce-scatter.7
